TPU v7x, 256 devices: a whole 4x4x8 slice. The times are simulated.
256 devices in a mesh: rep: 2 (over core), seq: 16 (over z, y_hi), head: 8 (over y_lo, x).
Axes of the slice: x: 4, y: 4 (y_hi: 2, y_lo: 2; y = y_hi * 2 + y_lo), z: 8, core: 2. Of those that a mesh axis runs over, the one named last changes fastest.
Arguments:
- query_latent: bfloat16 [2, 2048, 1536], P('rep', 'seq'), may hold values from -72 to 72
- kv_latent: bfloat16 [2, 2048, 576], P('rep', 'seq'), may hold values from -72 to 72
- query_up: bfloat16 [1536, 12288], P(None, 'head'), may hold values from -0.15625 to 0.15625
- kv_up: bfloat16 [512, 16384], P(None, 'head'), may hold values from -0.25 to 0.25
- out_grad: bfloat16 [2, 2048, 8192], P('rep', 'seq', 'head'), may hold values from -6 to 6
- positions: int32 [2, 2048], P('rep'), may hold values from 0 to 1535, as said below
Outputs:
- query_grad: bfloat16 [2, 2048, 1536], P('rep', 'seq')
- latent_grad: bfloat16 [2, 2048, 576], P('rep', ('seq', 'head'))
- query_up_grad: bfloat16 [1536, 12288], P(('rep', 'seq'), 'head')
Inputs may be any that keep to these rules, and one draw needn't show every extreme that they name: In each window, positions count tokens from the start of their document, rising by one a token and restarting at 0 where a document begins; a window's first token has position 0; the first document is exactly 1536 tokens long and no document is longer.
All inputs are finite; a program needn't handle non-finite values.
Results may differ from a plain program's by a relative error of at most 0.013.
The roundings to bfloat16 on the way count: a program that leaves them out, or rounds other values in their place, can miss the bound.
Values may be sent and summed in bfloat16 or wider, within the bound.
A program may use at most 128 MiB of HBM per device.

v0:
```python
import jax
import jax.numpy as jnp
from jax import lax
from jax.sharding import PartitionSpec as P

QL = 1536
KVL = 512
ROPE = 64
NOPE = 128
VD = 128


def rope_tables(positions):
    half_rope = ROPE // 2
    rotation_rates = 10000.0 ** (-jnp.arange(half_rope, dtype=jnp.float32) / half_rope)
    angles = positions.astype(jnp.float32)[:, None] * rotation_rates[None, :]
    return (jnp.cos(angles), jnp.sin(angles))


def rotate(vector, cosine, sine_table):
    half_rope = ROPE // 2
    front_half = vector[..., :half_rope]
    back_half = vector[..., half_rope:]
    return jnp.concatenate(
        [
            front_half * cosine - back_half * sine_table,
            front_half * sine_table + back_half * cosine,
        ],
        -1,
    )


def unrotate(vector, cosine, sine_table):
    half_rope = ROPE // 2
    front_half = vector[..., :half_rope]
    back_half = vector[..., half_rope:]
    return jnp.concatenate(
        [
            front_half * cosine + back_half * sine_table,
            back_half * cosine - front_half * sine_table,
        ],
        -1,
    )


def shards(query_latent, kv_latent, query_up, kv_up, out_grad, positions):
    tok_dev = query_latent.shape[1]
    heads_dev = query_up.shape[1] // (NOPE + ROPE)
    tokens = tok_dev * lax.axis_size("seq")
    first_row = lax.axis_index("seq") * tok_dev
    local_latent = query_latent[0]
    all_positions = positions[0]
    local_positions = lax.dynamic_slice_in_dim(all_positions, first_row, tok_dev)
    token_index = jnp.arange(tokens, dtype=jnp.int32)
    query_index = first_row + jnp.arange(tok_dev, dtype=jnp.int32)
    visible = (token_index[None, :] <= query_index[:, None]) & (
        local_positions[:, None] - all_positions[None, :]
        == query_index[:, None] - token_index[None, :]
    )
    cosine, sine_table = rope_tables(local_positions)
    softmax_scale = (NOPE + ROPE) ** (-0.5)
    query_weight = query_up.reshape(QL, heads_dev, NOPE + ROPE)
    kv_weight = kv_up.reshape(KVL, heads_dev, NOPE + VD)
    grad_heads = out_grad[0].reshape(tok_dev, heads_dev, VD).transpose(1, 0, 2)
    shard_rows = lax.all_gather(kv_latent[0], "seq", axis=0, tiled=True)
    projected = jnp.einsum(
        "tc,chd->htd", shard_rows[:, :KVL], kv_weight, preferred_element_type=jnp.float32
    )
    key_rope = jnp.broadcast_to(
        shard_rows[None, :, KVL:].astype(jnp.float32), (heads_dev, shard_rows.shape[0], ROPE)
    )
    key_value = jnp.concatenate(
        [projected[..., :NOPE], key_rope, projected[..., NOPE:]], -1
    ).astype(jnp.bfloat16)
    key_rows = key_value[..., : NOPE + ROPE]
    values = key_value[..., NOPE + ROPE :]
    projected_q = jnp.einsum(
        "tq,qhd->htd", local_latent, query_weight, preferred_element_type=jnp.float32
    )
    queries = jnp.concatenate(
        [projected_q[..., :NOPE], rotate(projected_q[..., NOPE:], cosine, sine_table)], -1
    ).astype(jnp.bfloat16)
    scores = (
        jnp.einsum("hqd,hkd->hqk", queries, key_rows, preferred_element_type=jnp.float32)
        * softmax_scale
    )
    scores = jnp.where(visible[None], scores, -jnp.inf)
    row_max = jnp.max(scores, 2, keepdims=True)
    exponent = jnp.exp(scores - row_max)
    attention = exponent / jnp.sum(exponent, 2, keepdims=True)
    prob_grad = jnp.einsum("hqd,hkd->hqk", grad_heads, values, preferred_element_type=jnp.float32)
    row_inner = jnp.sum(attention * prob_grad, 2, keepdims=True)
    score_grad = (attention * (prob_grad - row_inner) * softmax_scale).astype(jnp.bfloat16)
    attention_low = attention.astype(jnp.bfloat16)
    value_grad = jnp.einsum(
        "hqk,hqd->hkd", attention_low, grad_heads, preferred_element_type=jnp.float32
    ).astype(jnp.bfloat16)
    query_rows_grad = jnp.einsum(
        "hqk,hkd->hqd", score_grad, key_rows, preferred_element_type=jnp.float32
    )
    key_grad = jnp.einsum(
        "hqk,hqd->hkd", score_grad, queries, preferred_element_type=jnp.float32
    ).astype(jnp.bfloat16)
    head_query_grad = jnp.concatenate(
        [query_rows_grad[..., :NOPE], unrotate(query_rows_grad[..., NOPE:], cosine, sine_table)], -1
    ).astype(jnp.bfloat16)
    query_term = jnp.einsum(
        "htd,qhd->tq", head_query_grad, query_weight, preferred_element_type=jnp.float32
    )
    query_grad = lax.psum(query_term, "head").astype(jnp.bfloat16)[None]
    weight_term = jnp.einsum(
        "tq,htd->qhd", local_latent, head_query_grad, preferred_element_type=jnp.float32
    )
    weight_term = weight_term.reshape(QL, heads_dev * (NOPE + ROPE))
    kv_rows_grad = jnp.concatenate([key_grad[..., :NOPE], value_grad], -1)
    rope_grad = key_grad[..., NOPE:]
    latent_part = jnp.einsum(
        "htd,chd->tc", kv_rows_grad, kv_weight, preferred_element_type=jnp.float32
    )
    latent_grad = lax.psum_scatter(
        jnp.concatenate([latent_part, jnp.sum(rope_grad.astype(jnp.float32), 0)], -1),
        ("seq", "head"),
        scatter_dimension=0,
        tiled=True,
    )
    weight_grad = lax.psum_scatter(weight_term, ("rep", "seq"), scatter_dimension=0, tiled=True)
    return (query_grad, latent_grad.astype(jnp.bfloat16)[None], weight_grad.astype(jnp.bfloat16))


def solution(mesh):
    return jax.shard_map(
        shards,
        mesh=mesh,
        in_specs=(
            P("rep", "seq", None),
            P("rep", "seq", None),
            P(None, "head"),
            P(None, "head"),
            P("rep", "seq", "head"),
            P("rep", None),
        ),
        out_specs=(
            P("rep", "seq", None),
            P("rep", ("seq", "head"), None),
            P(("rep", "seq"), "head"),
        ),
        check_vma=False,
    )
```

profile of v0, /device:TPU:2, one launch (start us, length us, event | category | flops | bytes accessed | tf_op | source)
XLA Modules:
  0.0 1039.1 jit_solution(3629060452253005470)
XLA Ops:
  7.2 1.7 copy.33
  10.2 6.7 copy.32
  16.9 3.7 convolution_bitcast_fusion.1
  20.9 1.2 fusion.30
  22.1 80.6 %all-gather.3.cloned.1.call-done = bf16[1,2048,576]{2,1,0:T(8,128)(2,1)} async-done(((bf16[1,128,576]{2,1,0:T(8,128)(2,1)}), bf16[1,2048,576]{2,1,0:T(8,128)(2,1)}) %all-gather.3.cloned.1.call-update) | async-done | bytes 2359312 | tf_op jit(solution)/shard_map/all_gather | solution.py:65
  103.9 6.8 convert_bitcast_fusion
  111.2 4.5 fusion.12
  116.0 2.0 fusion.11
  118.1 5.7 fusion.47
  123.7 6.7 fusion.19
  130.4 15.9 %convolution_convert_fusion = bf16[8,2048,192]{1,2,0:T(8,128)(2,1)} fusion(f32[8,2048,128]{1,2,0:T(8,128)} %fusion.12, bf16[8,128,32]{1,2,0:T(8,128)(2,1)S(1)} %get-tuple-element.17, bf16[8,128,32]{1,2,0:T(8,128)(2,1)S(1)} %get-tuple-element.16, bf16[8,128,128]{1,2,0:T(8,128)(2,1)S(1)} %slice.89, f32[8,128,2048]{2,1,0:T(8,128)} %get-tuple-element.21, ...), kind=kOutput, calls=%fused_computation.19 | convolution fusion | flops 824314880 | bytes 23465984 | tf_op jit(solution)/shard_map/hqk,hqd->hkd/dot_general | solution.py:101
  146.3 2.1 convert_reduce_fusion
  149.8 1.2 copy-done.5
  151.0 4.5 fusion.23
  155.5 2.7 pad_maximum_fusion.3
  158.1 5.8 copy.49
  164.0 14.5 %fusion.10 = f32[8,128,192]{1,2,0:T(8,128)S(1)} fusion(bf16[8,2048,64]{1,2,0:T(8,128)(2,1)S(1)} %broadcast_in_dim.15, bf16[8,2048,128]{1,2,0:T(8,128)(2,1)} %copy-done.1, f32[8,2048,128]{1,2,0:T(8,128)} %fusion.12, f32[8,128,2048]{2,1,0:T(8,128)} %get-tuple-element.21, f32[8,128]{1,0:T(8,128)S(1)} %get-tuple-element.20), kind=kOutput, calls=%fused_computation.16 | convolution fusion | flops 832572416 | bytes 23859200 | tf_op jit(solution)/shard_map/hqk,hkd->hqd/dot_general | solution.py:98
  178.7 5.0 fusion.31
  183.7 9.6 copy.42
  193.4 3.2 convolution_bitcast_fusion
  196.5 38.2 %all-reduce.1 = bf16[128,1536]{1,0:T(8,128)(2,1)} all-reduce(f32[128,1536]{1,0:T(8,128)S(1)} %convolution_bitcast_fusion), channel_id=1, replica_groups=mesh['rep'=2,'seq'=16,'head'=8] {'head'}, use_global_device_ids=true, to_apply=%region_3.4 | all-reduce | flops 196608 | bytes 1179648 | tf_op jit(solution)/shard_map/psum | solution.py:110
  234.8 631.5 %reduce-scatter.7.cloned.1.call-done = f32[16,576]{1,0:T(8,128)} async-done(((f32[2048,576]{1,0:T(8,128)}), f32[16,576]{1,0:T(8,128)}) %reduce-scatter.7.cloned.1.call-update) | async-done | bytes 36880
  867.9 163.1 %reduce-scatter.5.cloned.1.call-done = f32[48,1536]{1,0:T(8,128)} async-done(((f32[1536,1536]{1,0:T(8,128)}), f32[48,1536]{1,0:T(8,128)}) %reduce-scatter.5.cloned.1.call-update) | async-done | bytes 294928 | tf_op jit(solution)/shard_map/reduce_scatter | solution.py:126
  1030.9 1.6 convert_element_type.44
  (34 shorter events, 6.6 us)
Async XLA Ops:
  7.2 9.7 copy-start
  7.2 95.4 %all-gather.3.cloned.1.call-start = ((), (), s32[]{:S(2)}) async-start(), calls=%async_computation.3 | async-start | bytes 2785280 | tf_op jit(solution)/shard_map/all_gather | solution.py:65
  9.0 857.2 %reduce-scatter.7.cloned.1.call-start = ((), (), s32[]{:S(2)}) async-start(), calls=%async_computation.4 | async-start | bytes 5283840
  10.2 10.5 %copy-start.3 = (s32[1,2048]{1,0:T(1,128)S(1)}, s32[1,2048]{1,0:T(1,128)}, u32[]{:S(2)}) copy-start(s32[1,2048]{1,0:T(1,128)} %param.11) | copy-start | bytes 24580
  111.2 4.8 copy-start.1
  116.0 2.0 copy-start.2
  146.3 2.8 slice-start
  146.3 3.5 copy-start.4
  146.3 4.7 copy-start.5
  164.0 867.0 %reduce-scatter.5.cloned.1.call-start = ((), (), s32[]{:S(2)}) async-start(), calls=%async_computation.2 | async-start | bytes 9732096 | tf_op jit(solution)/shard_map/reduce_scatter | solution.py:126
Sparse Core Ops, SparseCore 0:
  10.6 92.0 all-gather.2
  164.1 702.0 reduce-scatter.6
  870.7 160.2 reduce-scatter.4
where the time goes:
time: 1040 us
  waiting for transfers between devices  875 us (84%)
  matrix products  66.8 us (6%)
  blocking collectives  38.2 us (4%)
  local copies, waits for them, and re-layouts  31.3 us (3%)
  between operations  14 us (1%)
  other arithmetic  13.5 us (1%)
    unnamed x4, waiting for transfers between devices  632 us
    reduce_scatter x1, waiting for transfers between devices, shards(): lax.psum_scatter(weight_term, ('rep', 'seq'), scatter_dimension=0, tiled=...  163 us
    all_gather x1, waiting for transfers between devices, shards(): shard_rows = lax.all_gather(kv_latent[0], 'seq', axis=0, tiled=True)  80.6 us
    psum x1, blocking collectives, shards(): query_grad = lax.psum(query_term, 'head').astype(jnp.bfloat16)[None]  38.2 us
  transfers between devices with their start and end apart: 3, of which 3 were waited for; matrix products, arithmetic and copies ran while one was open for 5% of the time, Pallas kernels for 0%

commit v1 on v0

--- a/solution.py
+++ b/solution.py
@@ -107,7 +107,7 @@
     query_term = jnp.einsum(
         "htd,qhd->tq", head_query_grad, query_weight, preferred_element_type=jnp.float32
     )
-    query_grad = lax.psum(query_term, "head").astype(jnp.bfloat16)[None]
+    query_grad = jnp.sum(lax.all_gather(query_term, "head"), axis=0).astype(jnp.bfloat16)[None]
     weight_term = jnp.einsum(
         "tq,htd->qhd", local_latent, head_query_grad, preferred_element_type=jnp.float32
     )

time: 1040 us -> 1110 us (1.067)
  waiting for transfers between devices: 875 us -> 982 us
  blocking collectives: 38.2 us -> 0 us
    all_gather x0 -> x1, waiting for transfers between devices: none -> 71.6 us  [shards(): lax.all_gather(query_term, 'head')]
    psum x1 -> x0, blocking collectives: 38.2 us -> none  [shards(): query_grad = lax.psum(query_term, 'head').astype(jnp.bfloat16)[None]]
    unnamed x4 -> x5, waiting for transfers between devices: 632 us -> 669 us
  transfers between devices with their start and end apart: 3 -> 4, of which waited for: 3 -> 4; matrix products, arithmetic and copies ran while one was open for 5% -> 5% of each run, Pallas kernels for 0% -> 0%
where the time goes in v1:
time: 1110 us
  waiting for transfers between devices  982 us (88%)
  matrix products  68.1 us (6%)
  local copies, waits for them, and re-layouts  31.3 us (3%)
  other arithmetic  17.8 us (2%)
  between operations  14 us (1%)
    unnamed x5, waiting for transfers between devices  669 us
    reduce_scatter x1, waiting for transfers between devices, shards(): lax.psum_scatter(weight_term, ('rep', 'seq'), scatter_dimension=0, tiled=...  161 us
    all_gather x1, waiting for transfers between devices, shards(): shard_rows = lax.all_gather(kv_latent[0], 'seq', axis=0, tiled=True)  80.6 us
    all_gather x1, waiting for transfers between devices, shards(): lax.all_gather(query_term, 'head')  71.6 us
  transfers between devices with their start and end apart: 4, of which 4 were waited for; matrix products, arithmetic and copies ran while one was open for 5% of the time, Pallas kernels for 0%

profile of v1, /device:TPU:2, one launch (start us, length us, event | category | flops | bytes accessed | tf_op | source)
XLA Modules:
  0.0 1113.7 jit_solution(3270590368468296238)
XLA Ops:
  7.2 1.8 copy.33
  10.2 6.6 copy.32
  16.8 3.7 convolution_bitcast_fusion.1
  22.0 80.6 %all-gather.5.cloned.1.call-done = bf16[1,2048,576]{2,1,0:T(8,128)(2,1)} async-done(((bf16[1,128,576]{2,1,0:T(8,128)(2,1)}), bf16[1,2048,576]{2,1,0:T(8,128)(2,1)}) %all-gather.5.cloned.1.call-update) | async-done | bytes 2359312 | tf_op jit(solution)/shard_map/all_gather | solution.py:65
  103.9 6.8 convert_bitcast_fusion
  111.2 4.8 fusion.12
  116.3 2.0 fusion.11
  118.3 5.7 fusion.47
  124.0 6.7 fusion.19
  130.8 15.9 %convolution_convert_fusion = bf16[8,2048,192]{1,2,0:T(8,128)(2,1)} fusion(f32[8,2048,128]{1,2,0:T(8,128)} %fusion.12, bf16[8,128,32]{1,2,0:T(8,128)(2,1)S(1)} %get-tuple-element.17, bf16[8,128,32]{1,2,0:T(8,128)(2,1)S(1)} %get-tuple-element.16, bf16[8,128,128]{1,2,0:T(8,128)(2,1)S(1)} %slice.89, f32[8,128,2048]{2,1,0:T(8,128)} %get-tuple-element.21, ...), kind=kOutput, calls=%fused_computation.19 | convolution fusion | flops 824314880 | bytes 23465984 | tf_op jit(solution)/shard_map/hqk,hqd->hkd/dot_general | solution.py:101
  146.7 2.1 convert_reduce_fusion
  150.2 1.2 copy-done.5
  151.4 4.5 fusion.23
  155.9 2.7 pad_maximum_fusion.3
  158.6 5.9 copy.49
  164.5 14.7 %fusion.10 = f32[8,128,192]{1,2,0:T(8,128)S(1)} fusion(bf16[8,2048,64]{1,2,0:T(8,128)(2,1)S(1)} %broadcast_in_dim.13, bf16[8,2048,128]{1,2,0:T(8,128)(2,1)} %copy-done.1, f32[8,2048,128]{1,2,0:T(8,128)} %fusion.12, f32[8,128,2048]{2,1,0:T(8,128)} %get-tuple-element.21, f32[8,128]{1,0:T(8,128)S(1)} %get-tuple-element.20), kind=kOutput, calls=%fused_computation.16 | convolution fusion | flops 832572416 | bytes 23859200 | tf_op jit(solution)/shard_map/hqk,hkd->hqd/dot_general | solution.py:98
  179.3 4.1 convolution_bitcast_fusion
  183.4 5.0 fusion.31
  188.4 9.7 copy.42
  198.1 669.2 %reduce-scatter.7.cloned.1.call-done = f32[16,576]{1,0:T(8,128)} async-done(((f32[2048,576]{1,0:T(8,128)}), f32[16,576]{1,0:T(8,128)}) %reduce-scatter.7.cloned.1.call-update) | async-done | bytes 36880
  869.0 71.6 %all-gather.7.cloned.1.call-done = f32[1024,1536]{1,0:T(8,128)} async-done(((f32[128,1536]{1,0:T(8,128)}), f32[1024,1536]{1,0:T(8,128)}) %all-gather.7.cloned.1.call-update) | async-done | bytes 6291472 | tf_op jit(solution)/shard_map/all_gather | solution.py:110
  940.6 4.1 reduce_sum.38
  944.7 160.8 %reduce-scatter.5.cloned.1.call-done = f32[48,1536]{1,0:T(8,128)} async-done(((f32[1536,1536]{1,0:T(8,128)}), f32[48,1536]{1,0:T(8,128)}) %reduce-scatter.5.cloned.1.call-update) | async-done | bytes 294928 | tf_op jit(solution)/shard_map/reduce_scatter | solution.py:126
  1105.5 1.6 convert_element_type.55
  (37 shorter events, 7.9 us)
Async XLA Ops:
  7.2 9.7 copy-start
  7.2 95.4 %all-gather.5.cloned.1.call-start = ((), (), s32[]{:S(2)}) async-start(), calls=%async_computation.3 | async-start | bytes 2785280 | tf_op jit(solution)/shard_map/all_gather | solution.py:65
  9.0 858.3 %reduce-scatter.7.cloned.1.call-start = ((), (), s32[]{:S(2)}) async-start(), calls=%async_computation.5 | async-start | bytes 5283840
  10.2 10.4 copy-start.3
  111.2 5.0 copy-start.1
  116.3 2.0 copy-start.2
  146.7 2.8 slice-start
  146.7 3.5 copy-start.4
  146.7 4.7 copy-start.5
  164.5 776.1 %all-gather.7.cloned.1.call-start = ((), (), s32[]{:S(2)}) async-start(), calls=%async_computation.4 | async-start | bytes 7077888 | tf_op jit(solution)/shard_map/all_gather | solution.py:110
  183.4 922.1 %reduce-scatter.5.cloned.1.call-start = ((), (), s32[]{:S(2)}) async-start(), calls=%async_computation.2 | async-start | bytes 9732096 | tf_op jit(solution)/shard_map/reduce_scatter | solution.py:126
Sparse Core Ops, SparseCore 0:
  10.6 92.0 all-gather.4
  164.6 702.6 reduce-scatter.6
  869.1 71.3 all-gather.6
  944.9 160.5 reduce-scatter.4
